TPU v7x, 32 devices: a whole 2x2x4 slice. The times are simulated.
32 devices in a mesh: energy: 8 (over z, x), tile: 4 (over y, core).
Axes of the slice: x: 2, y: 2, z: 4, core: 2. Of those that a mesh axis runs over, the one named last changes fastest.
Arguments:
- object_tiles: float32 [8, 2, 4, 512, 512], P('energy', None, 'tile'), may hold values from -6 to 6
- probe_wave: float32 [8, 2, 256, 256], P('energy'), may hold values from -6 to 6
- measured: bfloat16 [8, 4, 16, 256, 256], P('energy', 'tile'), may hold values from 0 to 2
- positions: int32 [4, 16, 2], P('tile'), may hold values from 0 to 511, as said below
- materials: float32 [2, 8, 8], replicated, may hold values from -6 to 6
Outputs:
- fitted: float32 [8, 2, 4, 512, 512], P('energy', None, 'tile')
Inputs may be any that keep to these rules, and one draw needn't show every extreme that they name: `positions`: each entry is the corner of a 256 x 256 patch, given inside its tile; in every tile some patch has row corner 512 - 1 and some has column corner 512 - 1.
All inputs are finite; a program needn't handle non-finite values.
Results may differ from a plain program's by a relative error of at most 0.0013.
Values sent between devices are 32-bit elements; how exact they have to be, the bound alone decides.
A program may use at most 64 MiB of HBM per device.

v0:
```python
import functools
import math

import jax
import jax.numpy as jnp
import numpy as np
from jax import lax
from jax.experimental import pallas as pl
from jax.experimental.pallas import tpu as pltpu
from jax.sharding import PartitionSpec as P

TILE_COLS = 4
FIT_STEPS = 10
LANES = 128


amplitude_floor = 0.5


def shifted(value, axis, steps):
    count = lax.axis_size(axis)
    pairs = [(source, (source + steps) % count) for source in range(count)]
    return lax.ppermute(value, axis, pairs)


def fourier_parts(length):
    counter = np.arange(length, dtype=np.int64)
    angles = 2.0 * math.pi / length * (counter[:, None] * counter[None, :] % length)
    return jnp.asarray(
        np.stack([np.cos(angles), np.sin(angles)]).astype(np.float32).astype(jnp.bfloat16)
    )


def joined(top_left, top_right, bottom_left, bottom_right):
    return jnp.concatenate(
        [
            jnp.concatenate([top_left, top_right], 1),
            jnp.concatenate([bottom_left, bottom_right], 1),
        ],
        0,
    )


def transform(stacked, left_ref, right_ref):
    length = stacked.shape[0] // 2
    inner = jnp.dot(left_ref[...], stacked, preferred_element_type=jnp.float32)
    inner = inner.astype(jnp.bfloat16)
    beside = jnp.concatenate([inner[:length], inner[length:]], 1)
    outer = jnp.dot(beside, right_ref[...], preferred_element_type=jnp.float32) * (1.0 / length)
    return outer[:, :length], outer[:, length:]


def window(ref, part, row, block, shift, length):
    lane = lax.broadcasted_iota(jnp.int32, (length, LANES), 1)
    back = lax.rem(LANES - shift, LANES)
    tiles = [
        pltpu.roll(ref[part, block + at, pl.ds(row, length), :], back, 1)
        for at in range(length // LANES + 1)
    ]
    keep = lane < LANES - shift
    return jnp.concatenate(
        [jnp.where(keep, one, other) for one, other in zip(tiles[:-1], tiles[1:])], 1
    )


def add_window(ref, part, row, block, shift, term):
    length = term.shape[0]
    lane = lax.broadcasted_iota(jnp.int32, (length, LANES), 1)
    tiles = [pltpu.roll(term[:, at : at + LANES], shift, 1) for at in range(0, length, LANES)]
    keep = lane >= shift
    zero = jnp.zeros_like(tiles[0])
    for at, (one, other) in enumerate(zip(tiles + [zero], [zero] + tiles)):
        place = (part, block + at, pl.ds(row, length), slice(None))
        ref[place] = ref[place] + jnp.where(keep, one, other)


def patch_kernel(fold, inner, *refs):
    corners_ref, object_ref, measured_ref, probe_ref, fourier_ref = refs[:5]
    if inner:
        (gradient,) = refs[5:6]
        right_ref = lower_ref = None
        rest = refs[6:]
    else:
        right_ref, lower_ref, begun_ref, main_out, side_out, below_out = refs[5:11]
        gradient, *rest = refs[11:]
    field, tables, wave, change, terms, order, sems = rest
    tile_px = object_ref.shape[-1]
    length = probe_ref.shape[-1]
    count = measured_ref.shape[0]
    blocks = tile_px // LANES
    width = blocks + length // LANES
    top = pl.ds(0, tile_px)
    bottom = pl.ds(tile_px, length)
    moves = []
    for block in range(blocks if inner else width):
        ref, at = (object_ref, block) if block < blocks else (right_ref, block - blocks)
        columns = pl.ds(at * LANES, LANES)
        moves.append((ref.at[:, :, columns], field.at[:, block, top, :]))
        if fold and not inner and block < (tile_px - length) // LANES:
            continue
        if fold:
            source = ref.at[:, pl.ds(0, length), columns]
        elif not inner:
            source = lower_ref.at[:, :, pl.ds(block * LANES, LANES)]
        else:
            continue
        moves.append((source, field.at[:, block, bottom, :]))
    copies = [
        pltpu.make_async_copy(source, target, sems.at[number])
        for number, (source, target) in enumerate(moves)
    ]
    for copy in copies:
        copy.start()
    cosine = fourier_ref[0]
    sine = fourier_ref[1]
    tables[0] = joined(cosine, sine, -sine, cosine)
    tables[1] = joined(cosine, -sine, sine, cosine)
    if inner:
        gradient[...] = jnp.zeros_like(gradient)
    else:
        gradient[...] = begun_ref[...]
    terms[...] = jnp.zeros_like(terms)

    limit = tile_px - length

    def choose(number, found):
        order[found] = number
        within = corners_ref[number, 1] <= limit
        if not fold:
            within = jnp.logical_and(within, corners_ref[number, 0] <= limit)
        return found + jnp.where(within, int(inner), 1 - int(inner))

    total = lax.fori_loop(0, count, choose, 0)
    for copy in copies:
        copy.wait()

    def corner(turn):
        number = order[turn]
        row = corners_ref[number, 0]
        col = corners_ref[number, 1]
        block = col // LANES
        return number, row, block, col - block * LANES

    def gather(turn):
        _, row, block, shift = corner(turn)
        piece_real = window(field, 0, row, block, shift, length)
        piece_imag = window(field, 1, row, block, shift, length)
        probe_real = probe_ref[0]
        probe_imag = probe_ref[1]
        exit_real = probe_real * piece_real - probe_imag * piece_imag
        exit_imag = probe_real * piece_imag + probe_imag * piece_real
        wave[:length, :] = exit_real.astype(jnp.bfloat16)
        wave[length:, :] = exit_imag.astype(jnp.bfloat16)

    def scatter(turn):
        _, row, block, shift = corner(turn)
        add_window(gradient, 0, row, block, shift, terms[0])
        add_window(gradient, 1, row, block, shift, terms[1])

    def outward(turn):
        far_real, far_imag = transform(wave[...], tables.at[0], tables.at[1])
        square = far_real * far_real + far_imag * far_imag
        scale = lax.rsqrt(jnp.maximum(square, amplitude_floor * amplitude_floor))
        factor = measured_ref[order[turn]].astype(jnp.float32) * scale - 1.0
        return (factor * far_real).astype(jnp.bfloat16), (factor * far_imag).astype(jnp.bfloat16)

    def keep(parts):
        change[:length, :] = parts[0]
        change[length:, :] = parts[1]

    def homeward():
        back_real, back_imag = transform(change[...], tables.at[1], tables.at[0])
        probe_real = probe_ref[0]
        probe_imag = probe_ref[1]
        return (
            probe_real * back_real + probe_imag * back_imag,
            probe_real * back_imag - probe_imag * back_real,
        )

    def step(turn, carry):
        scatter(jnp.maximum(turn - 1, 0))
        parts = outward(turn + 1)
        back = homeward()
        keep(parts)
        gather(jnp.minimum(turn + 2, total - 1))
        terms[0] = back[0]
        terms[1] = back[1]
        return carry

    @pl.when(total > 0)
    def _():
        gather(0)
        keep(outward(0))
        gather(jnp.minimum(1, total - 1))
        lax.fori_loop(0, total - 1, step, 0)
        scatter(jnp.maximum(total - 2, 0))
        back = homeward()
        terms[0] = back[0]
        terms[1] = back[1]
        scatter(total - 1)

    if inner:
        return
    peak = jnp.max(probe_ref[0] * probe_ref[0] + probe_ref[1] * probe_ref[1])
    rows = 64

    def finish(wrapped, number, carry):
        place = (pl.ds(pl.multiple_of(number * rows, rows), rows), slice(None))
        beyond = pl.ds(pl.multiple_of(tile_px + number * rows, rows), rows)
        for part in range(2):
            for block in range(width):
                value = gradient[(part, block) + place]
                if wrapped:
                    value = value + gradient[part, block, beyond, :]
                share = value / peak
                if block < blocks:
                    columns = slice(block * LANES, (block + 1) * LANES)
                    main_out[part, place[0], columns] = field[(part, block) + place] + share
                else:
                    columns = slice((block - blocks) * LANES, (block - blocks + 1) * LANES)
                    side_out[part, place[0], columns] = share
        return carry

    lax.fori_loop(0, length // rows, functools.partial(finish, fold), 0)
    lax.fori_loop(length // rows, tile_px // rows, functools.partial(finish, False), 0)
    if fold:
        below_out[...] = jnp.zeros_like(below_out)
    else:
        for block in range(width):
            columns = slice(block * LANES, (block + 1) * LANES)
            below_out[:, :, columns] = gradient[:, block, tile_px:, :] / peak


def patch_call(own_object, probe, measured, corners, fold, margins=()):
    tile_px = own_object.shape[-1]
    length = probe.shape[-1]
    count = measured.shape[0]
    width = tile_px + length
    inner = not margins
    below = (2, 8, LANES) if fold else (2, length, width)
    vmem = pl.BlockSpec(memory_space=pltpu.VMEM)
    anywhere = pl.BlockSpec(memory_space=pl.ANY)
    sums = (2, width // LANES, width, LANES)
    if inner:
        shapes = [sums]
    else:
        shapes = [(2, tile_px, tile_px), (2, tile_px, length), below]
    scratch = [
        pltpu.VMEM(sums, jnp.float32),
        pltpu.VMEM((2, 2 * length, 2 * length), jnp.bfloat16),
        pltpu.VMEM((2 * length, length), jnp.bfloat16),
        pltpu.VMEM((2 * length, length), jnp.bfloat16),
        pltpu.VMEM((2, length, length), jnp.float32),
        pltpu.SMEM((count + 1,), jnp.int32),
        pltpu.SemaphoreType.DMA((2 * (width // LANES),)),
    ]
    if not inner:
        scratch = [pltpu.VMEM(sums, jnp.float32)] + scratch
    return pl.pallas_call(
        functools.partial(patch_kernel, fold, inner),
        out_shape=[jax.ShapeDtypeStruct(shape, jnp.float32) for shape in shapes],
        in_specs=[pl.BlockSpec(memory_space=pltpu.SMEM), anywhere, vmem, vmem, vmem]
        + ([] if inner else [anywhere, anywhere, vmem]),
        out_specs=[vmem] * len(shapes),
        scratch_shapes=scratch,
        compiler_params=pltpu.CompilerParams(vmem_limit_bytes=40 * 1024 * 1024),
        cost_estimate=pl.CostEstimate(
            flops=32 * count * length**3, bytes_accessed=16 * tile_px * tile_px, transcendentals=0
        ),
        name="patches_inner" if inner else "patches_outer",
    )(corners, own_object, measured, probe, fourier_parts(length), *margins)


def fit_scalars(materials_ref, energies, kinds):
    spectra = [
        [materials_ref[(part * energies + energy) * kinds + kind] for kind in range(kinds)]
        for part in range(2)
        for energy in range(energies)
    ]
    gram = [[None] * kinds for _ in range(kinds)]
    for one in range(kinds):
        for other in range(one, kinds):
            total = spectra[0][one] * spectra[0][other]
            for row in spectra[1:]:
                total = total + row[one] * row[other]
            gram[one][other] = total
            gram[other][one] = total
    trace = gram[0][0]
    for one in range(1, kinds):
        trace = trace + gram[one][one]
    return gram, trace


def fit_columns(materials_ref, step_ref, data, spectra, energies, kinds, rate, begin, wide):
    rows = data.shape[2]
    tall = 16 if rows % 16 == 0 else 8
    pairs = [(part, energy) for part in range(2) for energy in range(energies)]

    def chunk(number, carry):
        row = pl.multiple_of(number * tall, tall)
        place = (pl.ds(row, tall), pl.ds(begin, wide))
        target = [None] * kinds
        for part, energy in pairs:
            plane = data[(part, energy) + place]
            for kind in range(kinds):
                term = materials_ref[(part * energies + energy) * kinds + kind] * plane
                target[kind] = term if target[kind] is None else target[kind] + term
        target = [rate * value for value in target]
        current = [jnp.maximum(value, 0.0) for value in target]

        def descend(turn, current):
            following = []
            for one in range(kinds):
                total = target[one]
                for other in range(kinds):
                    total = total + step_ref[one * kinds + other] * current[other]
                following.append(jnp.maximum(total, 0.0))
            return following

        current = lax.fori_loop(1, FIT_STEPS, descend, current)
        for part, energy in pairs:
            total = None
            for kind in range(kinds):
                term = materials_ref[(part * energies + energy) * kinds + kind] * current[kind]
                total = term if total is None else total + term
            spectra[(part, energy) + place] = total
        return carry

    lax.fori_loop(0, rows // tall, chunk, 0)


def exchange_kernel(
    groups,
    tiles,
    materials_ref,
    main_ref,
    side_ref,
    out_ref,
    step_ref,
    margin,
    left,
    data,
    spectra,
    margin_sems,
    send_sems,
    recv_sems,
    own_sems,
):
    mesh_ids = pl.DeviceIdType.MESH
    me = lax.axis_index("energy")
    tile = lax.axis_index("tile")
    after = lax.rem(tile + 1, tiles)
    before = lax.rem(tile + tiles - 1, tiles)
    tile_px = main_ref.shape[-1]
    length = side_ref.shape[-1]
    rows = tile_px // groups
    kinds = materials_ref.shape[0] // (2 * groups)
    offsets = sorted(range(1, groups), key=lambda offset: abs(offset - groups // 2))
    peers = {offset: lax.rem(me + offset, groups) for offset in offsets}

    barrier = pltpu.get_barrier_semaphore()
    for neighbour in (after, before):
        pl.semaphore_signal(barrier, inc=1, device_id=(me, neighbour), device_id_type=mesh_ids)
    for offset in offsets:
        pl.semaphore_signal(
            barrier, inc=1, device_id=(peers[offset], tile), device_id_type=mesh_ids
        )

    pl.semaphore_wait(barrier, groups + 1)

    margin_copy = pltpu.make_async_remote_copy(
        src_ref=side_ref,
        dst_ref=margin,
        send_sem=margin_sems.at[0],
        recv_sem=margin_sems.at[1],
        device_id=(me, after),
        device_id_type=mesh_ids,
    )
    margin_copy.start()

    def rows_of(group):
        return pl.ds(pl.multiple_of(group * rows, rows), rows)

    def outward(block):
        columns = pl.ds(block * LANES, LANES)
        source = left if block * LANES < length else main_ref
        copies = [
            pltpu.make_async_remote_copy(
                src_ref=source.at[:, rows_of(peers[offset]), columns],
                dst_ref=data.at[:, me, :, columns],
                send_sem=send_sems.at[0, block, offset],
                recv_sem=recv_sems.at[0, block, offset],
                device_id=(peers[offset], tile),
                device_id_type=mesh_ids,
            )
            for offset in offsets
        ]
        own = pltpu.make_async_copy(
            source.at[:, rows_of(me), columns], data.at[:, me, :, columns], own_sems.at[0, block]
        )
        return copies, own

    def homeward(block):
        columns = pl.ds(block * LANES, LANES)
        copies = [
            pltpu.make_async_remote_copy(
                src_ref=spectra.at[:, peers[offset], :, columns],
                dst_ref=out_ref.at[:, rows_of(me), columns],
                send_sem=send_sems.at[1, block, offset],
                recv_sem=recv_sems.at[1, block, offset],
                device_id=(peers[offset], tile),
                device_id_type=mesh_ids,
            )
            for offset in offsets
        ]
        own = pltpu.make_async_copy(
            spectra.at[:, me, :, columns], out_ref.at[:, rows_of(me), columns], own_sems.at[1, block]
        )
        return copies, own

    def start(moves):
        for copy in moves[0]:
            copy.start()
        moves[1].start()

    blocks = tile_px // LANES
    early = [block for block in range(blocks) if block * LANES >= length]
    late = [block for block in range(blocks) if block * LANES < length]
    going = {}
    for block in early:
        going[block] = outward(block)
        start(going[block])

    gram, trace = fit_scalars(materials_ref, groups, kinds)
    rate = 1.0 / trace
    for one in range(kinds):
        for other in range(kinds):
            unit = 1.0 if one == other else 0.0
            step_ref[one * kinds + other] = unit - rate * gram[one][other]
    margin_copy.wait()
    for block in late:
        columns = slice(block * LANES, (block + 1) * LANES)
        left[:, :, columns] = main_ref[:, :, columns] + margin[:, :, columns]
    for block in late:
        going[block] = outward(block)
        start(going[block])
    coming = {}
    for block in early + late:
        copies, own = going[block]
        for copy in copies:
            copy.wait_recv()
        own.wait()
        fit_columns(
            materials_ref, step_ref, data, spectra, groups, kinds, rate, block * LANES, LANES
        )
        coming[block] = homeward(block)
        start(coming[block])
    for block in early + late:
        for copy in going[block][0]:
            copy.wait_send()
        copies, own = coming[block]
        own.wait()
        for copy in copies:
            copy.wait()


def exchange_fit(main, side, materials):
    groups = lax.axis_size("energy")
    tiles = lax.axis_size("tile")
    tile_px = main.shape[-1]
    length = side.shape[-1]
    kinds = materials.shape[-1]
    rows = tile_px // groups
    blocks = tile_px // LANES
    vmem = pl.BlockSpec(memory_space=pltpu.VMEM)
    return pl.pallas_call(
        functools.partial(exchange_kernel, groups, tiles),
        out_shape=jax.ShapeDtypeStruct(main.shape, jnp.float32),
        in_specs=[pl.BlockSpec(memory_space=pltpu.SMEM), vmem, vmem],
        out_specs=vmem,
        scratch_shapes=[
            pltpu.SMEM((kinds * kinds,), jnp.float32),
            pltpu.VMEM((2, tile_px, length), jnp.float32),
            pltpu.VMEM((2, tile_px, length), jnp.float32),
            pltpu.VMEM((2, groups, rows, tile_px), jnp.float32),
            pltpu.VMEM((2, groups, rows, tile_px), jnp.float32),
            pltpu.SemaphoreType.DMA((2,)),
            pltpu.SemaphoreType.DMA((2, blocks, groups)),
            pltpu.SemaphoreType.DMA((2, blocks, groups)),
            pltpu.SemaphoreType.DMA((2, blocks)),
        ],
        compiler_params=pltpu.CompilerParams(
            collective_id=0, has_side_effects=True, vmem_limit_bytes=32 * 1024 * 1024
        ),
        name="exchange",
    )(materials.reshape(-1), main, side)


def body(object_tiles, probe_wave, measured, positions, materials):
    own_object = object_tiles[0, :, 0]
    tile_px = own_object.shape[-1]
    length = probe_wave.shape[-1]
    tile_count = lax.axis_size("tile")
    row_step = TILE_COLS % tile_count
    fold = row_step == 0
    right_strip = shifted(own_object[:, :, :length], "tile", -1)
    if fold:
        lower_strip = jnp.zeros((2, 8, LANES), jnp.float32)
    else:
        widened = jnp.concatenate([own_object[:, :length], right_strip[:, :length]], 2)
        lower_strip = shifted(widened, "tile", -row_step)
    shared = (own_object, probe_wave[0], measured[0, 0], positions[0], fold)
    (begun,) = patch_call(*shared)
    main, side, below = patch_call(*shared, margins=(right_strip, lower_strip, begun))
    if not fold:
        from_above = shifted(below, "tile", row_step)
        main = main.at[:, :length, :].add(from_above[:, :, :tile_px])
        side = side.at[:, :length, :].add(from_above[:, :, tile_px:])
    fitted = exchange_fit(main, side, materials)
    return fitted.reshape(1, 2, 1, tile_px, tile_px)


def solution(mesh):
    in_specs = (
        P("energy", None, "tile", None, None),
        P("energy", None, None, None),
        P("energy", "tile", None, None, None),
        P("tile", None, None),
        P(),
    )
    out_specs = P("energy", None, "tile", None, None)
    return jax.shard_map(body, mesh=mesh, in_specs=in_specs, out_specs=out_specs, check_vma=False)
```

profile of v0, /device:TPU:0, one launch (start us, length us, event | category | flops | bytes accessed | tf_op | source)
XLA Modules:
  0.0 128.9 jit_solution(11001190589675163680)
XLA Ops:
  0.0 0.0 copy-start
  0.0 0.0 copy-start.5
  0.0 0.0 copy-start.4
  0.0 2.4 %slice.4 = f32[2,512,256]{2,1,0:T(8,128)} slice(f32[2,512,512]{2,1,0:T(8,128)} %bitcast.8), slice={[0:2], [0:512], [0:256]} | slice | bytes 2097152 | tf_op jit(solution)/shard_map/slice | solution.py:506
  2.4 2.4 %collective-permute-start = (f32[2,512,256]{2,1,0:T(8,128)}, f32[2,512,256]{2,1,0:T(8,128)S(1)}, u32[]{:S(2)}, u32[]{:S(2)}) collective-permute-start(f32[2,512,256]{2,1,0:T(8,128)} %slice.4), channel_id=1, source_target_pairs={{0,3},{1,0},{2,1},{3,2},{4,7},{5,4},{6,5},{7,6},{8,11},{9,8},{10,9... | collective-permute-start | bytes 3145736 | tf_op jit(solution)/shard_map/ppermute | solution.py:23
  4.9 0.0 copy-done.5
  4.9 0.1 copy.9.refs_0_
  4.9 0.0 copy-done.4
  4.9 0.1 reshape.6.materials_ref
  5.0 0.0 copy-done
  5.0 0.0 copy-start.1
  5.1 1.6 %copy-done.1 = bf16[1,1,16,256,256]{4,3,2,1,0:T(8,128)(2,1)S(1)} copy-done((bf16[1,1,16,256,256]{4,3,2,1,0:T(8,128)(2,1)S(1)}, bf16[1,1,16,256,256]{4,3,2,1,0:T(8,128)(2,1)}, u32[]{:S(2)}) %copy-start.1) | copy-done | bytes 2097176
  6.6 0.0 copy-start.2
  6.6 1.0 copy-done.2
  7.7 0.0 copy-start.3
  7.7 0.9 copy-done.3
  8.6 10.1 %patches_inner.1.refs_7_ = f32[2,6,768,128]{3,2,1,0:T(8,128)S(1)} custom-call(s32[16,2]{1,0:T(8,128)S(1)} %copy.9.refs_0_, f32[2,512,512]{2,1,0:T(8,128)S(1)} %bitcast.9, bf16[16,256,256]{2,1,0:T(8,128)(2,1)S(1)} %bitcast.11, f32[2,256,256]{2,1,0:T(8,128)S(1)} %bitcast.13, bf16[2,256,256]{2,1,0:T(8,128)(2,1)S(1)} %copy-done.3), custom_call_target="tpu_custom_call" | custom-call | flops 8589934592 | bytes 4194304 | tf_op jit(solution)/shard_map/patches_inner/pallas_call | solution.py:259
  18.8 0.0 collective-permute-done.refs_5_
  18.8 13.4 %patches_outer.1 = (f32[2,512,512]{2,1,0:T(8,128)S(1)}, f32[2,512,256]{2,1,0:T(8,128)S(1)}, f32[2,8,128]{2,1,0:T(8,128)}) custom-call(s32[16,2]{1,0:T(8,128)S(1)} %copy.9.refs_0_, f32[2,512,512]{2,1,0:T(8,128)S(1)} %bitcast.10, bf16[16,256,256]{2,1,0:T(8,128)(2,1)S(1)} %bitcast.12, f32[2,256,256]{2,1,0:T(8,128)S(1)} %bitcast.14, ...), custom_call_target="tpu_custom_call" | custom-call | flops 8589934592 | bytes 4194304 | tf_op jit(solution)/shard_map/patches_outer/pallas_call | solution.py:259
  32.2 95.3 %exchange.1 = f32[2,512,512]{2,1,0:T(8,128)S(1)} custom-call(f32[128]{0:T(128)S(1)} %reshape.6.materials_ref, f32[2,512,512]{2,1,0:T(8,128)S(1)} %get-tuple-element.7.main_ref, f32[2,512,256]{2,1,0:T(8,128)S(1)} %get-tuple-element.8.side_ref), custom_call_target="tpu_custom_call" | custom-call | tf_op jit(solution)/shard_map/exchange/pallas_call | solution.py:476
  127.6 1.3 %copy.12 = f32[1,2,1,512,512]{4,3,2,1,0:T(8,128)} copy(f32[1,2,1,512,512]{4,3,2,1,0:T(8,128)S(1)} %bitcast.7) | data formatting | bytes 4194304
  (1 shorter events, 0.0 us)
Async XLA Ops:
  0.0 5.0 %copy-start = (f32[1,2,1,512,512]{4,3,2,1,0:T(8,128)S(1)}, f32[1,2,1,512,512]{4,3,2,1,0:T(8,128)}, u32[]{:S(2)}) copy-start(f32[1,2,1,512,512]{4,3,2,1,0:T(8,128)} %param.7) | copy-start | bytes 6291460
  0.0 4.9 %copy-start.5 = (s32[1,16,2]{1,2,0:T(2,128)S(1)}, s32[1,16,2]{1,2,0:T(2,128)}, u32[]{:S(2)}) copy-start(s32[1,16,2]{1,2,0:T(2,128)} %param.10) | copy-start | bytes 388
  0.0 4.9 %copy-start.4 = (f32[2,8,8]{2,1,0:T(8,128)S(1)}, f32[2,8,8]{2,1,0:T(8,128)}, u32[]{:S(2)}) copy-start(f32[2,8,8]{2,1,0:T(8,128)} %param.11) | copy-start | bytes 1540
  2.4 16.3 %collective-permute-start = (f32[2,512,256]{2,1,0:T(8,128)}, f32[2,512,256]{2,1,0:T(8,128)S(1)}, u32[]{:S(2)}, u32[]{:S(2)}) collective-permute-start(f32[2,512,256]{2,1,0:T(8,128)} %slice.4), channel_id=1, source_target_pairs={{0,3},{1,0},{2,1},{3,2},{4,7},{5,4},{6,5},{7,6},{8,11},{9,8},{10,9... | collective-permute-start | bytes 3145736 | tf_op jit(solution)/shard_map/ppermute | solution.py:23
  5.0 1.6 %copy-start.1 = (bf16[1,1,16,256,256]{4,3,2,1,0:T(8,128)(2,1)S(1)}, bf16[1,1,16,256,256]{4,3,2,1,0:T(8,128)(2,1)}, u32[]{:S(2)}) copy-start(bf16[1,1,16,256,256]{4,3,2,1,0:T(8,128)(2,1)} %param.9) | copy-start | bytes 6291460
  6.6 1.0 copy-start.2
  7.7 0.9 copy-start.3
where the time goes:
time: 130 us; the launch traced here: 129 us
  Pallas kernels  119 us (92%)
  local copies, waits for them, and re-layouts  7.49 us (6%)
  starting transfers between devices  2.44 us (2%)
    pallas_call x1, Pallas kernels, exchange_fit(): pl.pallas_call(functools.partial(exchange_kernel, groups, tiles), out_sha...  95.3 us
    pallas_call x2, Pallas kernels, patch_call(): pl.pallas_call(functools.partial(patch_kernel, fold, inner), out_shape=[j...  23.5 us
    unnamed x13, local copies, waits for them, and re-layouts  4.91 us
  transfers between devices with their start and end apart: 1, of which 0 were waited for; matrix products, arithmetic and copies ran while one was open for 0% of the time, Pallas kernels for 8%

commit v1 on v0

--- a/solution.py
+++ b/solution.py
@@ -12,6 +12,7 @@
 TILE_COLS = 4
 FIT_STEPS = 10
 LANES = 128
+VMEM_LIMIT = 24 * 1024 * 1024
 
 
 amplitude_floor = 0.5
@@ -23,12 +24,16 @@
     return lax.ppermute(value, axis, pairs)
 
 
+def trig_parts(rows, columns, length):
+    angles = 2.0 * math.pi / length * (rows[:, None] * columns[None, :] % length)
+    return np.stack([np.cos(angles), np.sin(angles)]).astype(np.float32).astype(jnp.bfloat16)
+
+
 def fourier_parts(length):
     counter = np.arange(length, dtype=np.int64)
-    angles = 2.0 * math.pi / length * (counter[:, None] * counter[None, :] % length)
-    return jnp.asarray(
-        np.stack([np.cos(angles), np.sin(angles)]).astype(np.float32).astype(jnp.bfloat16)
-    )
+    half = counter[: length // 2]
+    left = np.stack([trig_parts(half, counter[parity::2], length) for parity in range(2)])
+    return jnp.asarray(left), jnp.asarray(trig_parts(counter, counter, length))
 
 
 def joined(top_left, top_right, bottom_left, bottom_right):
@@ -41,21 +46,23 @@
     )
 
 
-def transform(stacked, left_ref, right_ref):
-    length = stacked.shape[0] // 2
-    inner = jnp.dot(left_ref[...], stacked, preferred_element_type=jnp.float32)
-    inner = inner.astype(jnp.bfloat16)
-    beside = jnp.concatenate([inner[:length], inner[length:]], 1)
-    outer = jnp.dot(beside, right_ref[...], preferred_element_type=jnp.float32) * (1.0 / length)
+def transform(even, odd, left_ref, right_ref):
+    length = even.shape[0]
+    half = length // 2
+    one = jnp.dot(left_ref[0], even, preferred_element_type=jnp.float32)
+    two = jnp.dot(left_ref[1], odd, preferred_element_type=jnp.float32)
+    upper = (one + two).astype(jnp.bfloat16)
+    lower = (one - two).astype(jnp.bfloat16)
+    beside = joined(upper[:half], upper[half:], lower[:half], lower[half:])
+    outer = jnp.dot(beside, right_ref[...], preferred_element_type=jnp.float32)
     return outer[:, :length], outer[:, length:]
 
 
-def window(ref, part, row, block, shift, length):
-    lane = lax.broadcasted_iota(jnp.int32, (length, LANES), 1)
+def window(ref, part, rows, block, shift, length):
+    lane = lax.broadcasted_iota(jnp.int32, (rows.size, LANES), 1)
     back = lax.rem(LANES - shift, LANES)
     tiles = [
-        pltpu.roll(ref[part, block + at, pl.ds(row, length), :], back, 1)
-        for at in range(length // LANES + 1)
+        pltpu.roll(ref[part, block + at, rows, :], back, 1) for at in range(length // LANES + 1)
     ]
     keep = lane < LANES - shift
     return jnp.concatenate(
@@ -74,65 +81,111 @@
         ref[place] = ref[place] + jnp.where(keep, one, other)
 
 
-def patch_kernel(fold, inner, *refs):
-    corners_ref, object_ref, measured_ref, probe_ref, fourier_ref = refs[:5]
-    if inner:
-        (gradient,) = refs[5:6]
-        right_ref = lower_ref = None
-        rest = refs[6:]
+def patch_kernel(fold, phase, phases, *refs):
+    first = phase == 0
+    last = phase == phases - 1
+    if first:
+        corners_ref, object_ref, measured_ref, probe_ref, left_ref, right_ref = refs[:6]
+        gradient, field, wave, change, terms, held, left, right, probe, split = refs[6:16]
+        parts_left, parts_right, order, sems = refs[16:]
     else:
-        right_ref, lower_ref, begun_ref, main_out, side_out, below_out = refs[5:11]
-        gradient, *rest = refs[11:]
-    field, tables, wave, change, terms, order, sems = rest
-    tile_px = object_ref.shape[-1]
-    length = probe_ref.shape[-1]
-    count = measured_ref.shape[0]
-    blocks = tile_px // LANES
-    width = blocks + length // LANES
+        lower_count = 1 if last and not fold else 0
+        corners_ref, strip_ref = refs[:2]
+        lower_ref = refs[2] if lower_count else None
+        held, left, right, probe, split = refs[2 + lower_count : 7 + lower_count]
+        refs = refs[12 + lower_count :]
+        gradient, field, wave, change, terms = refs[:5]
+        if last:
+            main_out, side_out, below_out = refs[5:8]
+        order, sems = refs[-2:]
+    length = wave.shape[-1]
+    half = length // 2
+    pieces = length // LANES
+    width = field.shape[1]
+    blocks = width - pieces
+    tile_px = blocks * LANES
+    count = held.shape[0]
+    limit = tile_px - length
     top = pl.ds(0, tile_px)
     bottom = pl.ds(tile_px, length)
     moves = []
-    for block in range(blocks if inner else width):
-        ref, at = (object_ref, block) if block < blocks else (right_ref, block - blocks)
-        columns = pl.ds(at * LANES, LANES)
-        moves.append((ref.at[:, :, columns], field.at[:, block, top, :]))
-        if fold and not inner and block < (tile_px - length) // LANES:
-            continue
+    if first:
+        moves.append((left_ref, parts_left))
+        moves.append((right_ref, parts_right))
+        for block in range(blocks):
+            columns = pl.ds(block * LANES, LANES)
+            moves.append((object_ref.at[:, :, columns], field.at[:, block, top, :]))
+            if fold:
+                source = object_ref.at[:, pl.ds(0, length), columns]
+                moves.append((source, field.at[:, block, bottom, :]))
+        for piece in range(pieces):
+            columns = pl.ds(piece * LANES, LANES)
+            moves.append((probe_ref.at[:, :, columns], probe.at[:, piece]))
+        moves.append((measured_ref, held))
+    else:
+        block = blocks + phase - 1
+        moves.append((strip_ref, field.at[:, block, top, :]))
         if fold:
-            source = ref.at[:, pl.ds(0, length), columns]
-        elif not inner:
-            source = lower_ref.at[:, :, pl.ds(block * LANES, LANES)]
-        else:
-            continue
-        moves.append((source, field.at[:, block, bottom, :]))
+            moves.append((strip_ref.at[:, pl.ds(0, length), :], field.at[:, block, bottom, :]))
+        elif last:
+            for block in range(width):
+                columns = pl.ds(block * LANES, LANES)
+                moves.append((lower_ref.at[:, :, columns], field.at[:, block, bottom, :]))
     copies = [
         pltpu.make_async_copy(source, target, sems.at[number])
         for number, (source, target) in enumerate(moves)
     ]
     for copy in copies:
         copy.start()
-    cosine = fourier_ref[0]
-    sine = fourier_ref[1]
-    tables[0] = joined(cosine, sine, -sine, cosine)
-    tables[1] = joined(cosine, -sine, sine, cosine)
-    if inner:
+
+    def rank(number):
+        beyond = corners_ref[number, 1] - limit
+        kind = sum((beyond > step * LANES).astype(jnp.int32) for step in range(phases - 1))
+        if not fold:
+            kind = jnp.where(corners_ref[number, 0] > limit, phases - 1, kind)
+        return kind
+
+    kinds = [rank(number) for number in range(count)]
+    ends = [
+        sum((kind <= step).astype(jnp.int32) for kind in kinds) for step in range(phases)
+    ]
+    place = [jnp.int32(0)] + ends[:-1]
+    for number, kind in enumerate(kinds):
+        spot = place[-1]
+        for step in range(phases - 1):
+            spot = jnp.where(kind == step, place[step], spot)
+        order[spot] = number
+        place = [
+            value + (kind == step).astype(jnp.int32) for step, value in enumerate(place)
+        ]
+    begin = jnp.maximum(ends[phase - 1] - 2, 0) if phase else 0
+    end = count - 1 if last else jnp.maximum(ends[phase] - 2, 0)
+
+    if first:
         gradient[...] = jnp.zeros_like(gradient)
-    else:
-        gradient[...] = begun_ref[...]
-    terms[...] = jnp.zeros_like(terms)
-
-    limit = tile_px - length
-
-    def choose(number, found):
-        order[found] = number
-        within = corners_ref[number, 1] <= limit
-        if not fold:
-            within = jnp.logical_and(within, corners_ref[number, 0] <= limit)
-        return found + jnp.where(within, int(inner), 1 - int(inner))
-
-    total = lax.fori_loop(0, count, choose, 0)
+        terms[...] = jnp.zeros_like(terms)
+        for copy in copies[:2]:
+            copy.wait()
+        for parity in range(2):
+            cosine = parts_left[parity, 0]
+            sine = parts_left[parity, 1]
+            left[0, parity] = joined(cosine, sine, -sine, cosine)
+            left[1, parity] = joined(cosine, -sine, sine, cosine)
+        scale = jnp.asarray(1.0 / length, jnp.bfloat16)
+        cosine = parts_right[0] * scale
+        sine = parts_right[1] * scale
+        right[0] = joined(cosine, -sine, sine, cosine)
+        right[1] = joined(cosine, sine, -sine, cosine)
+        copies = copies[2:]
     for copy in copies:
         copy.wait()
+    if first:
+        for parity in range(2):
+            for part in range(2):
+                for piece in range(pieces):
+                    columns = slice(piece * LANES, (piece + 1) * LANES)
+                    rows = pl.ds(parity, half, stride=2)
+                    split[parity, part, :, columns] = probe[part, piece, rows, :]
 
     def corner(turn):
         number = order[turn]
@@ -143,14 +196,16 @@
 
     def gather(turn):
         _, row, block, shift = corner(turn)
-        piece_real = window(field, 0, row, block, shift, length)
-        piece_imag = window(field, 1, row, block, shift, length)
-        probe_real = probe_ref[0]
-        probe_imag = probe_ref[1]
-        exit_real = probe_real * piece_real - probe_imag * piece_imag
-        exit_imag = probe_real * piece_imag + probe_imag * piece_real
-        wave[:length, :] = exit_real.astype(jnp.bfloat16)
-        wave[length:, :] = exit_imag.astype(jnp.bfloat16)
+        for parity in range(2):
+            rows = pl.ds(row + parity, half, stride=2)
+            piece_real = window(field, 0, rows, block, shift, length)
+            piece_imag = window(field, 1, rows, block, shift, length)
+            probe_real = split[parity, 0]
+            probe_imag = split[parity, 1]
+            exit_real = probe_real * piece_real - probe_imag * piece_imag
+            exit_imag = probe_real * piece_imag + probe_imag * piece_real
+            wave[parity, :half, :] = exit_real.astype(jnp.bfloat16)
+            wave[parity, half:, :] = exit_imag.astype(jnp.bfloat16)
 
     def scatter(turn):
         _, row, block, shift = corner(turn)
@@ -158,20 +213,31 @@
         add_window(gradient, 1, row, block, shift, terms[1])
 
     def outward(turn):
-        far_real, far_imag = transform(wave[...], tables.at[0], tables.at[1])
+        far_real, far_imag = transform(wave[0], wave[1], left.at[0], right.at[0])
         square = far_real * far_real + far_imag * far_imag
         scale = lax.rsqrt(jnp.maximum(square, amplitude_floor * amplitude_floor))
-        factor = measured_ref[order[turn]].astype(jnp.float32) * scale - 1.0
-        return (factor * far_real).astype(jnp.bfloat16), (factor * far_imag).astype(jnp.bfloat16)
+        factor = held[order[turn]].astype(jnp.float32) * scale - 1.0
+        return factor * far_real, factor * far_imag
 
     def keep(parts):
-        change[:length, :] = parts[0]
-        change[length:, :] = parts[1]
+        for part in range(2):
+            for piece in range(pieces):
+                change[part, piece] = parts[part][:, piece * LANES : (piece + 1) * LANES]
+
+    def changed(parity):
+        rows = pl.ds(parity, half, stride=2)
+        return jnp.concatenate(
+            [
+                jnp.concatenate([change[part, piece, rows, :] for piece in range(pieces)], 1)
+                for part in range(2)
+            ],
+            0,
+        ).astype(jnp.bfloat16)
 
     def homeward():
-        back_real, back_imag = transform(change[...], tables.at[1], tables.at[0])
-        probe_real = probe_ref[0]
-        probe_imag = probe_ref[1]
+        back_real, back_imag = transform(changed(0), changed(1), left.at[1], right.at[1])
+        probe_real = jnp.concatenate([probe[0, piece] for piece in range(pieces)], 1)
+        probe_imag = jnp.concatenate([probe[1, piece] for piece in range(pieces)], 1)
         return (
             probe_real * back_real + probe_imag * back_imag,
             probe_real * back_imag - probe_imag * back_real,
@@ -182,37 +248,44 @@
         parts = outward(turn + 1)
         back = homeward()
         keep(parts)
-        gather(jnp.minimum(turn + 2, total - 1))
+        gather(jnp.minimum(turn + 2, count - 1))
         terms[0] = back[0]
         terms[1] = back[1]
         return carry
 
-    @pl.when(total > 0)
+    ready = ends[phase] >= 2
+    if not first:
+        ready = jnp.logical_and(ready, ends[phase - 1] < 2)
+
+    @pl.when(ready)
     def _():
         gather(0)
         keep(outward(0))
-        gather(jnp.minimum(1, total - 1))
-        lax.fori_loop(0, total - 1, step, 0)
-        scatter(jnp.maximum(total - 2, 0))
-        back = homeward()
-        terms[0] = back[0]
-        terms[1] = back[1]
-        scatter(total - 1)
-
-    if inner:
+        gather(1)
+
+    lax.fori_loop(begin, end, step, 0)
+    if not last:
         return
-    peak = jnp.max(probe_ref[0] * probe_ref[0] + probe_ref[1] * probe_ref[1])
-    rows = 64
+    scatter(count - 2)
+    back = homeward()
+    terms[0] = back[0]
+    terms[1] = back[1]
+    scatter(count - 1)
+
+    peak = jnp.max(probe[0] * probe[0] + probe[1] * probe[1])
+    inverse = 1.0 / jnp.full((8, LANES), peak, jnp.float32)
+    tall = 64
+    inverse = jnp.concatenate([inverse] * (tall // 8), 0)
 
     def finish(wrapped, number, carry):
-        place = (pl.ds(pl.multiple_of(number * rows, rows), rows), slice(None))
-        beyond = pl.ds(pl.multiple_of(tile_px + number * rows, rows), rows)
+        place = (pl.ds(pl.multiple_of(number * tall, tall), tall), slice(None))
+        beyond = pl.ds(pl.multiple_of(tile_px + number * tall, tall), tall)
         for part in range(2):
             for block in range(width):
                 value = gradient[(part, block) + place]
                 if wrapped:
                     value = value + gradient[part, block, beyond, :]
-                share = value / peak
+                share = value * inverse
                 if block < blocks:
                     columns = slice(block * LANES, (block + 1) * LANES)
                     main_out[part, place[0], columns] = field[(part, block) + place] + share
@@ -221,54 +294,90 @@
                     side_out[part, place[0], columns] = share
         return carry
 
-    lax.fori_loop(0, length // rows, functools.partial(finish, fold), 0)
-    lax.fori_loop(length // rows, tile_px // rows, functools.partial(finish, False), 0)
+    lax.fori_loop(0, length // tall, functools.partial(finish, fold), 0)
+    lax.fori_loop(length // tall, tile_px // tall, functools.partial(finish, False), 0)
     if fold:
         below_out[...] = jnp.zeros_like(below_out)
     else:
         for block in range(width):
             columns = slice(block * LANES, (block + 1) * LANES)
-            below_out[:, :, columns] = gradient[:, block, tile_px:, :] / peak
-
-
-def patch_call(own_object, probe, measured, corners, fold, margins=()):
+            below_out[:, :, columns] = gradient[:, block, tile_px:, :] * inverse[:1]
+
+
+def patch_calls(own_object, probe, measured, corners, fold, strips, lower):
     tile_px = own_object.shape[-1]
     length = probe.shape[-1]
     count = measured.shape[0]
     width = tile_px + length
-    inner = not margins
-    below = (2, 8, LANES) if fold else (2, length, width)
+    pieces = length // LANES
+    phases = 1 + len(strips)
     vmem = pl.BlockSpec(memory_space=pltpu.VMEM)
     anywhere = pl.BlockSpec(memory_space=pl.ANY)
+    smem = pl.BlockSpec(memory_space=pltpu.SMEM)
+    single = jnp.float32
+    brief = jnp.bfloat16
     sums = (2, width // LANES, width, LANES)
-    if inner:
-        shapes = [sums]
-    else:
-        shapes = [(2, tile_px, tile_px), (2, tile_px, length), below]
-    scratch = [
-        pltpu.VMEM(sums, jnp.float32),
-        pltpu.VMEM((2, 2 * length, 2 * length), jnp.bfloat16),
-        pltpu.VMEM((2 * length, length), jnp.bfloat16),
-        pltpu.VMEM((2 * length, length), jnp.bfloat16),
-        pltpu.VMEM((2, length, length), jnp.float32),
-        pltpu.SMEM((count + 1,), jnp.int32),
-        pltpu.SemaphoreType.DMA((2 * (width // LANES),)),
-    ]
-    if not inner:
-        scratch = [pltpu.VMEM(sums, jnp.float32)] + scratch
-    return pl.pallas_call(
-        functools.partial(patch_kernel, fold, inner),
-        out_shape=[jax.ShapeDtypeStruct(shape, jnp.float32) for shape in shapes],
-        in_specs=[pl.BlockSpec(memory_space=pltpu.SMEM), anywhere, vmem, vmem, vmem]
-        + ([] if inner else [anywhere, anywhere, vmem]),
-        out_specs=[vmem] * len(shapes),
-        scratch_shapes=scratch,
-        compiler_params=pltpu.CompilerParams(vmem_limit_bytes=40 * 1024 * 1024),
-        cost_estimate=pl.CostEstimate(
-            flops=32 * count * length**3, bytes_accessed=16 * tile_px * tile_px, transcendentals=0
-        ),
-        name="patches_inner" if inner else "patches_outer",
-    )(corners, own_object, measured, probe, fourier_parts(length), *margins)
+    moving = [
+        jax.ShapeDtypeStruct(sums, single),
+        jax.ShapeDtypeStruct(sums, single),
+        jax.ShapeDtypeStruct((2, length, length), brief),
+        jax.ShapeDtypeStruct((2, pieces, length, LANES), single),
+        jax.ShapeDtypeStruct((2, length, length), single),
+    ]
+    fixed = [
+        jax.ShapeDtypeStruct(measured.shape, brief),
+        jax.ShapeDtypeStruct((2, 2, length, length), brief),
+        jax.ShapeDtypeStruct((2, 2 * length, 2 * length), brief),
+        jax.ShapeDtypeStruct((2, pieces, length, LANES), single),
+        jax.ShapeDtypeStruct((2, 2, length // 2, length), single),
+    ]
+    below = (2, 8, LANES) if fold else (2, length, width)
+    results = [
+        jax.ShapeDtypeStruct(shape, single)
+        for shape in [(2, tile_px, tile_px), (2, tile_px, length), below]
+    ]
+    parts_left, parts_right = fourier_parts(length)
+    shared = [
+        pltpu.SMEM((count,), jnp.int32),
+        pltpu.SemaphoreType.DMA((3 + 3 * (width // LANES),)),
+    ]
+    params = pltpu.CompilerParams(vmem_limit_bytes=VMEM_LIMIT)
+    cost = pl.CostEstimate(
+        flops=8 * count * length**3, bytes_accessed=8 * tile_px * tile_px, transcendentals=0
+    )
+    state = pl.pallas_call(
+        functools.partial(patch_kernel, fold, 0, phases),
+        out_shape=moving + fixed,
+        in_specs=[smem] + [anywhere] * 5,
+        out_specs=[vmem] * len(moving + fixed),
+        scratch_shapes=[
+            pltpu.VMEM(parts_left.shape, brief),
+            pltpu.VMEM(parts_right.shape, brief),
+        ]
+        + shared,
+        compiler_params=params,
+        cost_estimate=cost,
+        name="patches_0",
+    )(corners, own_object, measured, probe, parts_left, parts_right)
+    held = state[len(moving) :]
+    state = state[: len(moving)]
+    for phase, strip in enumerate(strips, 1):
+        last = phase == phases - 1
+        more = [lower] if last and not fold else []
+        lead = 2 + len(more) + len(held)
+        out = pl.pallas_call(
+            functools.partial(patch_kernel, fold, phase, phases),
+            out_shape=moving + (results if last else []),
+            in_specs=[smem] + [anywhere] * (1 + len(more)) + [vmem] * len(held + state),
+            out_specs=[vmem] * (len(moving) + (len(results) if last else 0)),
+            scratch_shapes=shared,
+            input_output_aliases={lead + at: at for at in range(len(moving))},
+            compiler_params=params,
+            cost_estimate=cost,
+            name=f"patches_{phase}",
+        )(corners, strip, *more, *held, *state)
+        state = out[: len(moving)]
+    return out[len(moving) :]
 
 
 def fit_scalars(materials_ref, energies, kinds):
@@ -503,15 +612,17 @@
     tile_count = lax.axis_size("tile")
     row_step = TILE_COLS % tile_count
     fold = row_step == 0
-    right_strip = shifted(own_object[:, :, :length], "tile", -1)
-    if fold:
-        lower_strip = jnp.zeros((2, 8, LANES), jnp.float32)
-    else:
-        widened = jnp.concatenate([own_object[:, :length], right_strip[:, :length]], 2)
+    chunks = [own_object[:, :, at : at + LANES] for at in range(0, length, LANES)]
+    strips = [shifted(chunk, "tile", -1) for chunk in chunks]
+    lower_strip = None
+    if not fold:
+        widened = jnp.concatenate(
+            [own_object[:, :length]] + [strip[:, :length] for strip in strips], 2
+        )
         lower_strip = shifted(widened, "tile", -row_step)
-    shared = (own_object, probe_wave[0], measured[0, 0], positions[0], fold)
-    (begun,) = patch_call(*shared)
-    main, side, below = patch_call(*shared, margins=(right_strip, lower_strip, begun))
+    main, side, below = patch_calls(
+        own_object, probe_wave[0], measured[0, 0], positions[0], fold, strips, lower_strip
+    )
     if not fold:
         from_above = shifted(below, "tile", row_step)
         main = main.at[:, :length, :].add(from_above[:, :, :tile_px])

time: 130 us -> 126 us (0.969); the launches traced: 129 us -> 126 us
  Pallas kernels: 119 us -> 115 us
    pallas_call x2 -> x3, Pallas kernels: 23.5 us -> 19.6 us  [the longest x2 12.4 us: patch_calls(): pl.pallas_call(functools.partial(patch_kernel, fold, phase, phases), out_...]
    unnamed x13 -> x15, local copies, waits for them, and re-layouts: 4.91 us -> 5.81 us
    ppermute x1 -> x2, starting transfers between devices: 2.44 us -> 3.11 us  [shifted(): return lax.ppermute(value, axis, pairs)]
  transfers between devices with their start and end apart: 1 -> 2, of which waited for: 0 -> 0; matrix products, arithmetic and copies ran while one was open for 0% -> 0% of each run, Pallas kernels for 8% -> 9%
where the time goes in v1:
time: 126 us
  Pallas kernels  115 us (91%)
  local copies, waits for them, and re-layouts  8.38 us (7%)
  starting transfers between devices  3.11 us (2%)
    pallas_call x1, Pallas kernels, exchange_fit(): pl.pallas_call(functools.partial(exchange_kernel, groups, tiles), out_sha...  95.1 us
    pallas_call x2, Pallas kernels, patch_calls(): pl.pallas_call(functools.partial(patch_kernel, fold, phase, phases), out_...  12.4 us
    pallas_call x1, Pallas kernels, patch_calls(): pl.pallas_call(functools.partial(patch_kernel, fold, 0, phases), out_shap...  7.23 us
    unnamed x15, local copies, waits for them, and re-layouts  5.81 us
    ppermute x2, starting transfers between devices, shifted(): return lax.ppermute(value, axis, pairs)  3.11 us
  transfers between devices with their start and end apart: 2, of which 0 were waited for; matrix products, arithmetic and copies ran while one was open for 0% of the time, Pallas kernels for 9%

profile of v1, /device:TPU:0, one launch (start us, length us, event | category | flops | bytes accessed | tf_op | source)
XLA Modules:
  0.0 126.3 jit_solution(6819456758765427826)
XLA Ops:
  0.0 0.0 copy-start
  0.0 0.0 copy-start.6
  0.0 0.0 copy-start.5
  0.0 2.4 %fusion = (f32[2,512,128]{2,1,0:T(8,128)}, f32[2,512,128]{2,1,0:T(8,128)}) fusion(f32[2,512,512]{2,1,0:T(8,128)} %bitcast.8), kind=kLoop, calls=%fused_computation | loop fusion | bytes 2097152 | tf_op jit(solution)/shard_map/slice | solution.py:615
  2.4 2.4 %collective-permute-start.1 = (f32[2,512,128]{2,1,0:T(8,128)}, f32[2,512,128]{2,1,0:T(8,128)S(1)}, u32[]{:S(2)}, u32[]{:S(2)}) collective-permute-start(f32[2,512,128]{2,1,0:T(8,128)} %get-tuple-element.39), channel_id=1, source_target_pairs={{0,3},{1,0},{2,1},{3,2},{4,7},{5,4},{6,5},{7,6},{8,11},{9,8},{10,9... | collective-permute-start | bytes 1572872 | tf_op jit(solution)/shard_map/ppermute | solution.py:24
  4.8 0.7 collective-permute-start
  5.5 0.0 copy-done.6
  5.5 0.1 copy.20.refs_0_
  5.6 0.0 copy-done.5
  5.6 0.1 reshape.6.materials_ref
  5.7 0.0 copy-done
  5.7 0.0 copy-start.1
  5.7 1.6 %copy-done.1 = bf16[1,1,16,256,256]{4,3,2,1,0:T(8,128)(2,1)S(1)} copy-done((bf16[1,1,16,256,256]{4,3,2,1,0:T(8,128)(2,1)S(1)}, bf16[1,1,16,256,256]{4,3,2,1,0:T(8,128)(2,1)}, u32[]{:S(2)}) %copy-start.1) | copy-done | bytes 2097176
  7.3 0.0 copy-start.2
  7.3 1.0 copy-done.2
  8.3 0.0 copy-start.3
  8.3 0.9 copy-done.3
  9.3 0.0 copy-start.4
  9.3 0.9 copy-done.4
  10.2 7.2 %patches_0.1 = (f32[2,6,768,128]{3,2,1,0:T(8,128)S(1)}, f32[2,6,768,128]{3,2,1,0:T(8,128)S(1)}, bf16[2,256,256]{2,1,0:T(8,128)(2,1)S(1)}, f32[2,2,256,128]{3,2,1...) custom-call(s32[16,2]{1,0:T(8,128)S(1)} %copy.20.refs_0_, ...), custom_call_target="tpu_custom_call" | custom-call | flops 2147483648 | bytes 2097152 | tf_op jit(solution)/shard_map/patches_0/pallas_call | solution.py:348
  17.4 0.0 collective-permute-done.1.refs_1_
  17.5 3.7 %patches_1.1 = (f32[2,6,768,128]{3,2,1,0:T(8,128)S(1)}, f32[2,6,768,128]{3,2,1,0:T(8,128)S(1)}, bf16[2,256,256]{2,1,0:T(8,128)(2,1)S(1)}, f32[2,2,256,128]{3,2,1,0:T(8,128)S(1)}, f32[2,256,256]{2,1,0:T(8,128)S(1)}) custom-call(s32[16,2]{1,0:T(8,128)S(1)} %copy.20.refs_0_, ...), custom_call_target="tpu_custom_call", output_to_operand_aliasing={{0}: (7, {}), {1}: (8, {}), {2}: (9, {}), {3}: (10, {}), {4... | custom-call | flops 2147483648 | bytes 2097152 | tf_op jit(solution)/shard_map/patches_1/pallas_call | solution.py:368
  21.1 0.0 collective-permute-done.refs_1_
  21.1 8.7 %patches_2.1 = (f32[2,6,768,128]{3,2,1,0:T(8,128)S(1)}, f32[2,6,768,128]{3,2,1,0:T(8,128)S(1)}, bf16[2,256,256]{2,1,0:T(8,128)(2,1)S(1)}, f32[2,2,256,128]{3,2,1...) custom-call(s32[16,2]{1,0:T(8,128)S(1)} %copy.20.refs_0_, ...), custom_call_target="tpu_custom_call", output_to_operand_aliasing={{0}: (7, {}), {1}: (8, {}), {2}: (9, {}), {3}: (10, {}), {4... | custom-call | flops 2147483648 | bytes 2097152 | tf_op jit(solution)/shard_map/patches_2/pallas_call | solution.py:368
  29.9 95.1 %exchange.1 = f32[2,512,512]{2,1,0:T(8,128)S(1)} custom-call(f32[128]{0:T(128)S(1)} %reshape.6.materials_ref, f32[2,512,512]{2,1,0:T(8,128)S(1)} %get-tuple-element.37.main_ref, f32[2,512,256]{2,1,0:T(8,128)S(1)} %get-tuple-element.38.side_ref), custom_call_target="tpu_custom_call" | custom-call | tf_op jit(solution)/shard_map/exchange/pallas_call | solution.py:585
  125.0 1.3 %copy.33 = f32[1,2,1,512,512]{4,3,2,1,0:T(8,128)} copy(f32[1,2,1,512,512]{4,3,2,1,0:T(8,128)S(1)} %bitcast.7) | data formatting | bytes 4194304
Async XLA Ops:
  0.0 5.7 %copy-start = (f32[1,2,1,512,512]{4,3,2,1,0:T(8,128)S(1)}, f32[1,2,1,512,512]{4,3,2,1,0:T(8,128)}, u32[]{:S(2)}) copy-start(f32[1,2,1,512,512]{4,3,2,1,0:T(8,128)} %param.7) | copy-start | bytes 6291460
  0.0 5.5 %copy-start.6 = (s32[1,16,2]{1,2,0:T(2,128)S(1)}, s32[1,16,2]{1,2,0:T(2,128)}, u32[]{:S(2)}) copy-start(s32[1,16,2]{1,2,0:T(2,128)} %param.10) | copy-start | bytes 388
  0.0 5.6 %copy-start.5 = (f32[2,8,8]{2,1,0:T(8,128)S(1)}, f32[2,8,8]{2,1,0:T(8,128)}, u32[]{:S(2)}) copy-start(f32[2,8,8]{2,1,0:T(8,128)} %param.11) | copy-start | bytes 1540
  2.4 15.0 %collective-permute-start.1 = (f32[2,512,128]{2,1,0:T(8,128)}, f32[2,512,128]{2,1,0:T(8,128)S(1)}, u32[]{:S(2)}, u32[]{:S(2)}) collective-permute-start(f32[2,512,128]{2,1,0:T(8,128)} %get-tuple-element.39), channel_id=1, source_target_pairs={{0,3},{1,0},{2,1},{3,2},{4,7},{5,4},{6,5},{7,6},{8,11},{9,8},{10,9... | collective-permute-start | bytes 1572872 | tf_op jit(solution)/shard_map/ppermute | solution.py:24
  4.8 16.3 %collective-permute-start = (f32[2,512,128]{2,1,0:T(8,128)}, f32[2,512,128]{2,1,0:T(8,128)S(1)}, u32[]{:S(2)}, u32[]{:S(2)}) collective-permute-start(f32[2,512,128]{2,1,0:T(8,128)} %get-tuple-element.40), channel_id=1, source_target_pairs={{0,3},{1,0},{2,1},{3,2},{4,7},{5,4},{6,5},{7,6},{8,11},{9,8},{10,9... | collective-permute-start | bytes 1572872 | tf_op jit(solution)/shard_map/ppermute | solution.py:24
  5.7 1.6 %copy-start.1 = (bf16[1,1,16,256,256]{4,3,2,1,0:T(8,128)(2,1)S(1)}, bf16[1,1,16,256,256]{4,3,2,1,0:T(8,128)(2,1)}, u32[]{:S(2)}) copy-start(bf16[1,1,16,256,256]{4,3,2,1,0:T(8,128)(2,1)} %param.9) | copy-start | bytes 6291460
  7.3 1.0 copy-start.2
  8.3 0.9 copy-start.3
  9.3 0.9 copy-start.4

commit v2 on v1

--- a/solution.py
+++ b/solution.py
@@ -12,7 +12,8 @@
 TILE_COLS = 4
 FIT_STEPS = 10
 LANES = 128
-VMEM_LIMIT = 24 * 1024 * 1024
+VMEM_LIMIT = 12 * 1024 * 1024
+LOAD_LIMIT = 8 * 1024 * 1024
 
 
 amplitude_floor = 0.5
@@ -81,23 +82,73 @@
         ref[place] = ref[place] + jnp.where(keep, one, other)
 
 
+def load_kernel(fold, object_ref, probe_ref, left_ref, right_ref, *refs):
+    *strips, gradient, field, terms, left, right, probe, split = refs[:-3]
+    parts_left, parts_right, sems = refs[-3:]
+    length = probe_ref.shape[-1]
+    half = length // 2
+    pieces = length // LANES
+    tile_px = object_ref.shape[-1]
+    top = pl.ds(0, tile_px)
+    bottom = pl.ds(tile_px, length)
+    moves = [(left_ref, parts_left), (right_ref, parts_right)]
+    for piece, strip in enumerate(strips):
+        moves.append((object_ref.at[:, :, pl.ds(piece * LANES, LANES)], strip))
+    for piece in range(pieces):
+        columns = pl.ds(piece * LANES, LANES)
+        moves.append((probe_ref.at[:, :, columns], probe.at[:, piece]))
+    for block in range(tile_px // LANES):
+        columns = pl.ds(block * LANES, LANES)
+        moves.append((object_ref.at[:, :, columns], field.at[:, block, top, :]))
+        if fold:
+            source = object_ref.at[:, pl.ds(0, length), columns]
+            moves.append((source, field.at[:, block, bottom, :]))
+    copies = [
+        pltpu.make_async_copy(source, target, sems.at[number])
+        for number, (source, target) in enumerate(moves)
+    ]
+    for copy in copies:
+        copy.start()
+    gradient[...] = jnp.zeros_like(gradient)
+    terms[...] = jnp.zeros_like(terms)
+    for copy in copies[:2]:
+        copy.wait()
+    for parity in range(2):
+        cosine = parts_left[parity, 0]
+        sine = parts_left[parity, 1]
+        left[0, parity] = joined(cosine, sine, -sine, cosine)
+        left[1, parity] = joined(cosine, -sine, sine, cosine)
+    scale = jnp.asarray(1.0 / length, jnp.bfloat16)
+    cosine = parts_right[0] * scale
+    sine = parts_right[1] * scale
+    right[0] = joined(cosine, -sine, sine, cosine)
+    right[1] = joined(cosine, sine, -sine, cosine)
+    early = 2 + len(strips) + pieces
+    for copy in copies[2:early]:
+        copy.wait()
+    for parity in range(2):
+        for part in range(2):
+            for piece in range(pieces):
+                columns = slice(piece * LANES, (piece + 1) * LANES)
+                rows = pl.ds(parity, half, stride=2)
+                split[parity, part, :, columns] = probe[part, piece, rows, :]
+    for copy in copies[early:]:
+        copy.wait()
+
+
 def patch_kernel(fold, phase, phases, *refs):
     first = phase == 0
     last = phase == phases - 1
-    if first:
-        corners_ref, object_ref, measured_ref, probe_ref, left_ref, right_ref = refs[:6]
-        gradient, field, wave, change, terms, held, left, right, probe, split = refs[6:16]
-        parts_left, parts_right, order, sems = refs[16:]
-    else:
-        lower_count = 1 if last and not fold else 0
-        corners_ref, strip_ref = refs[:2]
-        lower_ref = refs[2] if lower_count else None
-        held, left, right, probe, split = refs[2 + lower_count : 7 + lower_count]
-        refs = refs[12 + lower_count :]
-        gradient, field, wave, change, terms = refs[:5]
-        if last:
-            main_out, side_out, below_out = refs[5:8]
-        order, sems = refs[-2:]
+    lower_count = 1 if last and not fold else 0
+    strip_count = 0 if first else 1
+    lead = 1 + lower_count + strip_count
+    corners_ref = refs[0]
+    strip_ref = None if first else refs[1]
+    lower_ref = refs[2] if lower_count else None
+    held, left, right, probe, split = refs[lead : lead + 5]
+    refs = refs[lead + 5 + (3 if first else 5) :]
+    gradient, field, terms, wave, change = refs[:5]
+    order, sems = refs[-2:]
     length = wave.shape[-1]
     half = length // 2
     pieces = length // LANES
@@ -109,20 +160,7 @@
     top = pl.ds(0, tile_px)
     bottom = pl.ds(tile_px, length)
     moves = []
-    if first:
-        moves.append((left_ref, parts_left))
-        moves.append((right_ref, parts_right))
-        for block in range(blocks):
-            columns = pl.ds(block * LANES, LANES)
-            moves.append((object_ref.at[:, :, columns], field.at[:, block, top, :]))
-            if fold:
-                source = object_ref.at[:, pl.ds(0, length), columns]
-                moves.append((source, field.at[:, block, bottom, :]))
-        for piece in range(pieces):
-            columns = pl.ds(piece * LANES, LANES)
-            moves.append((probe_ref.at[:, :, columns], probe.at[:, piece]))
-        moves.append((measured_ref, held))
-    else:
+    if not first:
         block = blocks + phase - 1
         moves.append((strip_ref, field.at[:, block, top, :]))
         if fold:
@@ -139,10 +177,10 @@
         copy.start()
 
     def rank(number):
-        beyond = corners_ref[number, 1] - limit
+        beyond = corners_ref[1, number] - limit
         kind = sum((beyond > step * LANES).astype(jnp.int32) for step in range(phases - 1))
         if not fold:
-            kind = jnp.where(corners_ref[number, 0] > limit, phases - 1, kind)
+            kind = jnp.where(corners_ref[0, number] > limit, phases - 1, kind)
         return kind
 
     kinds = [rank(number) for number in range(count)]
@@ -160,37 +198,13 @@
         ]
     begin = jnp.maximum(ends[phase - 1] - 2, 0) if phase else 0
     end = count - 1 if last else jnp.maximum(ends[phase] - 2, 0)
-
-    if first:
-        gradient[...] = jnp.zeros_like(gradient)
-        terms[...] = jnp.zeros_like(terms)
-        for copy in copies[:2]:
-            copy.wait()
-        for parity in range(2):
-            cosine = parts_left[parity, 0]
-            sine = parts_left[parity, 1]
-            left[0, parity] = joined(cosine, sine, -sine, cosine)
-            left[1, parity] = joined(cosine, -sine, sine, cosine)
-        scale = jnp.asarray(1.0 / length, jnp.bfloat16)
-        cosine = parts_right[0] * scale
-        sine = parts_right[1] * scale
-        right[0] = joined(cosine, -sine, sine, cosine)
-        right[1] = joined(cosine, sine, -sine, cosine)
-        copies = copies[2:]
     for copy in copies:
         copy.wait()
-    if first:
-        for parity in range(2):
-            for part in range(2):
-                for piece in range(pieces):
-                    columns = slice(piece * LANES, (piece + 1) * LANES)
-                    rows = pl.ds(parity, half, stride=2)
-                    split[parity, part, :, columns] = probe[part, piece, rows, :]
 
     def corner(turn):
         number = order[turn]
-        row = corners_ref[number, 0]
-        col = corners_ref[number, 1]
+        row = corners_ref[0, number]
+        col = corners_ref[1, number]
         block = col // LANES
         return number, row, block, col - block * LANES
 
@@ -264,125 +278,98 @@
         gather(1)
 
     lax.fori_loop(begin, end, step, 0)
-    if not last:
-        return
-    scatter(count - 2)
-    back = homeward()
-    terms[0] = back[0]
-    terms[1] = back[1]
-    scatter(count - 1)
-
-    peak = jnp.max(probe[0] * probe[0] + probe[1] * probe[1])
-    inverse = 1.0 / jnp.full((8, LANES), peak, jnp.float32)
-    tall = 64
-    inverse = jnp.concatenate([inverse] * (tall // 8), 0)
-
-    def finish(wrapped, number, carry):
-        place = (pl.ds(pl.multiple_of(number * tall, tall), tall), slice(None))
-        beyond = pl.ds(pl.multiple_of(tile_px + number * tall, tall), tall)
-        for part in range(2):
-            for block in range(width):
-                value = gradient[(part, block) + place]
-                if wrapped:
-                    value = value + gradient[part, block, beyond, :]
-                share = value * inverse
-                if block < blocks:
-                    columns = slice(block * LANES, (block + 1) * LANES)
-                    main_out[part, place[0], columns] = field[(part, block) + place] + share
-                else:
-                    columns = slice((block - blocks) * LANES, (block - blocks + 1) * LANES)
-                    side_out[part, place[0], columns] = share
-        return carry
-
-    lax.fori_loop(0, length // tall, functools.partial(finish, fold), 0)
-    lax.fori_loop(length // tall, tile_px // tall, functools.partial(finish, False), 0)
-    if fold:
-        below_out[...] = jnp.zeros_like(below_out)
-    else:
-        for block in range(width):
-            columns = slice(block * LANES, (block + 1) * LANES)
-            below_out[:, :, columns] = gradient[:, block, tile_px:, :] * inverse[:1]
-
-
-def patch_calls(own_object, probe, measured, corners, fold, strips, lower):
+    if last:
+        scatter(count - 2)
+        back = homeward()
+        terms[0] = back[0]
+        terms[1] = back[1]
+        scatter(count - 1)
+
+
+def patch_calls(own_object, probe, measured, corners, fold, shift):
     tile_px = own_object.shape[-1]
     length = probe.shape[-1]
     count = measured.shape[0]
     width = tile_px + length
     pieces = length // LANES
-    phases = 1 + len(strips)
+    phases = 1 + pieces
     vmem = pl.BlockSpec(memory_space=pltpu.VMEM)
     anywhere = pl.BlockSpec(memory_space=pl.ANY)
     smem = pl.BlockSpec(memory_space=pltpu.SMEM)
-    single = jnp.float32
-    brief = jnp.bfloat16
+
+    def single(*shape):
+        return jax.ShapeDtypeStruct(shape, jnp.float32)
+
+    def brief(*shape):
+        return jax.ShapeDtypeStruct(shape, jnp.bfloat16)
+
     sums = (2, width // LANES, width, LANES)
     moving = [
-        jax.ShapeDtypeStruct(sums, single),
-        jax.ShapeDtypeStruct(sums, single),
-        jax.ShapeDtypeStruct((2, length, length), brief),
-        jax.ShapeDtypeStruct((2, pieces, length, LANES), single),
-        jax.ShapeDtypeStruct((2, length, length), single),
+        single(*sums),
+        single(*sums),
+        single(2, length, length),
+        brief(2, length, length),
+        single(2, pieces, length, LANES),
     ]
     fixed = [
-        jax.ShapeDtypeStruct(measured.shape, brief),
-        jax.ShapeDtypeStruct((2, 2, length, length), brief),
-        jax.ShapeDtypeStruct((2, 2 * length, 2 * length), brief),
-        jax.ShapeDtypeStruct((2, pieces, length, LANES), single),
-        jax.ShapeDtypeStruct((2, 2, length // 2, length), single),
+        brief(2, 2, length, length),
+        brief(2, 2 * length, 2 * length),
+        single(2, pieces, length, LANES),
+        single(2, 2, length // 2, length),
     ]
-    below = (2, 8, LANES) if fold else (2, length, width)
-    results = [
-        jax.ShapeDtypeStruct(shape, single)
-        for shape in [(2, tile_px, tile_px), (2, tile_px, length), below]
-    ]
+    loaded = [single(2, tile_px, LANES)] * pieces + moving[:3] + fixed
     parts_left, parts_right = fourier_parts(length)
-    shared = [
-        pltpu.SMEM((count,), jnp.int32),
-        pltpu.SemaphoreType.DMA((3 + 3 * (width // LANES),)),
-    ]
-    params = pltpu.CompilerParams(vmem_limit_bytes=VMEM_LIMIT)
-    cost = pl.CostEstimate(
-        flops=8 * count * length**3, bytes_accessed=8 * tile_px * tile_px, transcendentals=0
-    )
-    state = pl.pallas_call(
-        functools.partial(patch_kernel, fold, 0, phases),
-        out_shape=moving + fixed,
-        in_specs=[smem] + [anywhere] * 5,
-        out_specs=[vmem] * len(moving + fixed),
+    sources = (own_object, probe, parts_left, parts_right)
+    out = pl.pallas_call(
+        functools.partial(load_kernel, fold),
+        out_shape=loaded,
+        in_specs=[anywhere] * 4,
+        out_specs=[vmem] * len(loaded),
         scratch_shapes=[
-            pltpu.VMEM(parts_left.shape, brief),
-            pltpu.VMEM(parts_right.shape, brief),
-        ]
-        + shared,
-        compiler_params=params,
-        cost_estimate=cost,
-        name="patches_0",
-    )(corners, own_object, measured, probe, parts_left, parts_right)
-    held = state[len(moving) :]
-    state = state[: len(moving)]
-    for phase, strip in enumerate(strips, 1):
+            pltpu.VMEM(parts_left.shape, jnp.bfloat16),
+            pltpu.VMEM(parts_right.shape, jnp.bfloat16),
+            pltpu.SemaphoreType.DMA((2 + 2 * pieces + 2 * (tile_px // LANES),)),
+        ],
+        compiler_params=pltpu.CompilerParams(vmem_limit_bytes=LOAD_LIMIT),
+        cost_estimate=pl.CostEstimate(flops=10**10, bytes_accessed=2**24, transcendentals=0),
+        name="load",
+    )(*(pltpu.with_memory_space_constraint(value, pltpu.HBM) for value in sources))
+    strips = [shift(strip) for strip in out[:pieces]]
+    state = list(out[pieces : pieces + 3])
+    held = [measured, *out[pieces + 3 :]]
+    for phase in range(phases):
         last = phase == phases - 1
-        more = [lower] if last and not fold else []
-        lead = 2 + len(more) + len(held)
-        out = pl.pallas_call(
+        more = [strips[phase - 1]] if phase else []
+        if last and not fold:
+            widened = jnp.concatenate(
+                [own_object[:, :length]] + [strip[:, :length] for strip in strips], 2
+            )
+            more.append(shifted(widened, "tile", -(TILE_COLS % lax.axis_size("tile"))))
+        lead = 1 + len(more) + len(held)
+        state = pl.pallas_call(
             functools.partial(patch_kernel, fold, phase, phases),
-            out_shape=moving + (results if last else []),
-            in_specs=[smem] + [anywhere] * (1 + len(more)) + [vmem] * len(held + state),
-            out_specs=[vmem] * (len(moving) + (len(results) if last else 0)),
-            scratch_shapes=shared,
-            input_output_aliases={lead + at: at for at in range(len(moving))},
-            compiler_params=params,
-            cost_estimate=cost,
+            out_shape=moving,
+            in_specs=[smem] + [anywhere] * len(more) + [vmem] * (len(held) + len(state)),
+            out_specs=[vmem] * len(moving),
+            scratch_shapes=[
+                pltpu.SMEM((count,), jnp.int32),
+                pltpu.SemaphoreType.DMA((2 + width // LANES,)),
+            ],
+            input_output_aliases={lead + at: at for at in range(len(state))},
+            compiler_params=pltpu.CompilerParams(vmem_limit_bytes=VMEM_LIMIT),
+            cost_estimate=pl.CostEstimate(
+                flops=8 * count * length**3,
+                bytes_accessed=8 * tile_px * tile_px,
+                transcendentals=0,
+            ),
             name=f"patches_{phase}",
-        )(corners, strip, *more, *held, *state)
-        state = out[: len(moving)]
-    return out[len(moving) :]
+        )(corners, *more, *held, *state)
+    return state[0], state[1], held[3]
 
 
 def fit_scalars(materials_ref, energies, kinds):
     spectra = [
-        [materials_ref[(part * energies + energy) * kinds + kind] for kind in range(kinds)]
+        [materials_ref[part, energy, kind] for kind in range(kinds)]
         for part in range(2)
         for energy in range(energies)
     ]
@@ -412,7 +399,7 @@
         for part, energy in pairs:
             plane = data[(part, energy) + place]
             for kind in range(kinds):
-                term = materials_ref[(part * energies + energy) * kinds + kind] * plane
+                term = materials_ref[part, energy, kind] * plane
                 target[kind] = term if target[kind] is None else target[kind] + term
         target = [rate * value for value in target]
         current = [jnp.maximum(value, 0.0) for value in target]
@@ -430,7 +417,7 @@
         for part, energy in pairs:
             total = None
             for kind in range(kinds):
-                term = materials_ref[(part * energies + energy) * kinds + kind] * current[kind]
+                term = materials_ref[part, energy, kind] * current[kind]
                 total = term if total is None else total + term
             spectra[(part, energy) + place] = total
         return carry
@@ -441,13 +428,16 @@
 def exchange_kernel(
     groups,
     tiles,
+    fold,
     materials_ref,
-    main_ref,
-    side_ref,
+    gradient,
+    field,
+    probe,
     out_ref,
     step_ref,
+    main,
+    side,
     margin,
-    left,
     data,
     spectra,
     margin_sems,
@@ -460,10 +450,11 @@
     tile = lax.axis_index("tile")
     after = lax.rem(tile + 1, tiles)
     before = lax.rem(tile + tiles - 1, tiles)
-    tile_px = main_ref.shape[-1]
-    length = side_ref.shape[-1]
+    tile_px = out_ref.shape[-1]
+    length = probe.shape[2]
+    blocks = tile_px // LANES
     rows = tile_px // groups
-    kinds = materials_ref.shape[0] // (2 * groups)
+    kinds = materials_ref.shape[2]
     offsets = sorted(range(1, groups), key=lambda offset: abs(offset - groups // 2))
     peers = {offset: lax.rem(me + offset, groups) for offset in offsets}
 
@@ -475,10 +466,32 @@
             barrier, inc=1, device_id=(peers[offset], tile), device_id_type=mesh_ids
         )
 
+    peak = jnp.max(probe[0] * probe[0] + probe[1] * probe[1])
+    tall = 64
+    inverse = 1.0 / jnp.full((tall, LANES), peak, jnp.float32)
+
+    def finish(wrapped, number, carry):
+        place = (pl.ds(pl.multiple_of(number * tall, tall), tall), slice(None))
+        beyond = pl.ds(pl.multiple_of(tile_px + number * tall, tall), tall)
+        for part in range(2):
+            for block in range(field.shape[1]):
+                value = gradient[(part, block) + place]
+                if wrapped:
+                    value = value + gradient[part, block, beyond, :]
+                share = value * inverse
+                if block < blocks:
+                    main[(part, block) + place] = field[(part, block) + place] + share
+                else:
+                    side[(part, block - blocks) + place] = share
+        return carry
+
+    lax.fori_loop(0, length // tall, functools.partial(finish, fold), 0)
+    lax.fori_loop(length // tall, tile_px // tall, functools.partial(finish, False), 0)
+
     pl.semaphore_wait(barrier, groups + 1)
 
     margin_copy = pltpu.make_async_remote_copy(
-        src_ref=side_ref,
+        src_ref=side,
         dst_ref=margin,
         send_sem=margin_sems.at[0],
         recv_sem=margin_sems.at[1],
@@ -492,10 +505,9 @@
 
     def outward(block):
         columns = pl.ds(block * LANES, LANES)
-        source = left if block * LANES < length else main_ref
         copies = [
             pltpu.make_async_remote_copy(
-                src_ref=source.at[:, rows_of(peers[offset]), columns],
+                src_ref=main.at[:, block, rows_of(peers[offset]), :],
                 dst_ref=data.at[:, me, :, columns],
                 send_sem=send_sems.at[0, block, offset],
                 recv_sem=recv_sems.at[0, block, offset],
@@ -505,7 +517,7 @@
             for offset in offsets
         ]
         own = pltpu.make_async_copy(
-            source.at[:, rows_of(me), columns], data.at[:, me, :, columns], own_sems.at[0, block]
+            main.at[:, block, rows_of(me), :], data.at[:, me, :, columns], own_sems.at[0, block]
         )
         return copies, own
 
@@ -532,7 +544,6 @@
             copy.start()
         moves[1].start()
 
-    blocks = tile_px // LANES
     early = [block for block in range(blocks) if block * LANES >= length]
     late = [block for block in range(blocks) if block * LANES < length]
     going = {}
@@ -548,8 +559,7 @@
             step_ref[one * kinds + other] = unit - rate * gram[one][other]
     margin_copy.wait()
     for block in late:
-        columns = slice(block * LANES, (block + 1) * LANES)
-        left[:, :, columns] = main_ref[:, :, columns] + margin[:, :, columns]
+        main[:, block] = main[:, block] + margin[:, block]
     for block in late:
         going[block] = outward(block)
         start(going[block])
@@ -573,24 +583,25 @@
             copy.wait()
 
 
-def exchange_fit(main, side, materials):
+def exchange_fit(gradient, field, probe, materials, fold):
     groups = lax.axis_size("energy")
     tiles = lax.axis_size("tile")
-    tile_px = main.shape[-1]
-    length = side.shape[-1]
+    pieces = probe.shape[1]
+    blocks = field.shape[1] - pieces
+    tile_px = blocks * LANES
     kinds = materials.shape[-1]
     rows = tile_px // groups
-    blocks = tile_px // LANES
     vmem = pl.BlockSpec(memory_space=pltpu.VMEM)
     return pl.pallas_call(
-        functools.partial(exchange_kernel, groups, tiles),
-        out_shape=jax.ShapeDtypeStruct(main.shape, jnp.float32),
-        in_specs=[pl.BlockSpec(memory_space=pltpu.SMEM), vmem, vmem],
+        functools.partial(exchange_kernel, groups, tiles, fold),
+        out_shape=jax.ShapeDtypeStruct((2, tile_px, tile_px), jnp.float32),
+        in_specs=[pl.BlockSpec(memory_space=pltpu.SMEM), vmem, vmem, vmem],
         out_specs=vmem,
         scratch_shapes=[
             pltpu.SMEM((kinds * kinds,), jnp.float32),
-            pltpu.VMEM((2, tile_px, length), jnp.float32),
-            pltpu.VMEM((2, tile_px, length), jnp.float32),
+            pltpu.VMEM((2, blocks, tile_px, LANES), jnp.float32),
+            pltpu.VMEM((2, pieces, tile_px, LANES), jnp.float32),
+            pltpu.VMEM((2, pieces, tile_px, LANES), jnp.float32),
             pltpu.VMEM((2, groups, rows, tile_px), jnp.float32),
             pltpu.VMEM((2, groups, rows, tile_px), jnp.float32),
             pltpu.SemaphoreType.DMA((2,)),
@@ -599,35 +610,30 @@
             pltpu.SemaphoreType.DMA((2, blocks)),
         ],
         compiler_params=pltpu.CompilerParams(
-            collective_id=0, has_side_effects=True, vmem_limit_bytes=32 * 1024 * 1024
+            collective_id=0, has_side_effects=True, vmem_limit_bytes=24 * 1024 * 1024
         ),
         name="exchange",
-    )(materials.reshape(-1), main, side)
+    )(materials, gradient, field, probe)
 
 
 def body(object_tiles, probe_wave, measured, positions, materials):
     own_object = object_tiles[0, :, 0]
     tile_px = own_object.shape[-1]
     length = probe_wave.shape[-1]
-    tile_count = lax.axis_size("tile")
-    row_step = TILE_COLS % tile_count
+    row_step = TILE_COLS % lax.axis_size("tile")
     fold = row_step == 0
-    chunks = [own_object[:, :, at : at + LANES] for at in range(0, length, LANES)]
-    strips = [shifted(chunk, "tile", -1) for chunk in chunks]
-    lower_strip = None
-    if not fold:
-        widened = jnp.concatenate(
-            [own_object[:, :length]] + [strip[:, :length] for strip in strips], 2
-        )
-        lower_strip = shifted(widened, "tile", -row_step)
-    main, side, below = patch_calls(
-        own_object, probe_wave[0], measured[0, 0], positions[0], fold, strips, lower_strip
+    gradient, field, probe = patch_calls(
+        own_object,
+        probe_wave[0],
+        measured[0, 0],
+        positions[0].T,
+        fold,
+        functools.partial(shifted, axis="tile", steps=-1),
     )
     if not fold:
-        from_above = shifted(below, "tile", row_step)
-        main = main.at[:, :length, :].add(from_above[:, :, :tile_px])
-        side = side.at[:, :length, :].add(from_above[:, :, tile_px:])
-    fitted = exchange_fit(main, side, materials)
+        from_above = shifted(gradient[:, :, tile_px:], "tile", row_step)
+        gradient = gradient.at[:, :, :length].add(from_above)
+    fitted = exchange_fit(gradient, field, probe, materials, fold)
     return fitted.reshape(1, 2, 1, tile_px, tile_px)
 
 

time: 126 us -> 124 us (0.984)
  local copies, waits for them, and re-layouts: 8.38 us -> 1.33 us
  waiting for transfers between devices: 0.01 us -> 4.92 us
    ppermute x2, waiting for transfers between devices: 0.01 us -> 4.92 us  [shifted(): return lax.ppermute(value, axis, pairs)]
    pallas_call x2, Pallas kernels: 102 us -> 97.8 us  [the longest x1 95 us: exchange_fit(): pl.pallas_call(functools.partial(exchange_kernel, groups, tiles, fold), o...]
    unnamed x15 -> x7, local copies, waits for them, and re-layouts: 5.81 us -> 1.33 us
    pallas_call x2 -> x3, Pallas kernels: 12.4 us -> 16.7 us  [patch_calls(): pl.pallas_call(functools.partial(patch_kernel, fold, phase, phases), out_...]
    slice x1 -> x0, local copies, waits for them, and re-layouts: 2.4 us -> none  [body(): chunks = [own_object[:, :, at:at + LANES] for at in range(0, length, LANES)]]
  transfers between devices with their start and end apart: 2 -> 2, of which waited for: 0 -> 2; matrix products, arithmetic and copies ran while one was open for 0% -> 0% of each run, Pallas kernels for 9% -> 5%
where the time goes in v2:
time: 124 us
  Pallas kernels  114 us (92%)
  waiting for transfers between devices  4.92 us (4%)
  starting transfers between devices  3.16 us (3%)
  local copies, waits for them, and re-layouts  1.33 us (1%)
    pallas_call x1, Pallas kernels, exchange_fit(): pl.pallas_call(functools.partial(exchange_kernel, groups, tiles, fold), o...  95 us
    pallas_call x3, Pallas kernels, patch_calls(): pl.pallas_call(functools.partial(patch_kernel, fold, phase, phases), out_...  16.7 us
    ppermute x2, waiting for transfers between devices, shifted(): return lax.ppermute(value, axis, pairs)  4.92 us
    ppermute x2, starting transfers between devices, shifted(): return lax.ppermute(value, axis, pairs)  3.16 us
    pallas_call x1, Pallas kernels, patch_calls(): pl.pallas_call(functools.partial(load_kernel, fold), out_shape=loaded, in...  2.78 us
  transfers between devices with their start and end apart: 2, of which 2 were waited for; matrix products, arithmetic and copies ran while one was open for 0% of the time, Pallas kernels for 5%

profile of v2, /device:TPU:0, one launch (start us, length us, event | category | flops | bytes accessed | tf_op | source)
XLA Modules:
  0.0 124.0 jit_solution(155919769555337168)
XLA Ops:
  0.0 0.0 copy-start
  0.0 0.0 copy-start.1
  0.0 2.8 %load.1 = (f32[2,512,128]{2,1,0:T(8,128)S(1)}, f32[2,512,128]{2,1,0:T(8,128)S(1)}, f32[2,6,768,128]{3,2,1,0:T(8,128)S(1)}, f32[2,6,768,128]{3,2,1,0:T(8,128)S(1)...) custom-call(f32[2,512,512]{2,1,0:T(8,128)} %bitcast.16, ...), custom_call_target="tpu_custom_call" | custom-call | flops 10000000000 | bytes 16777216 | tf_op jit(solution)/shard_map/load/pallas_call | solution.py:323
  2.8 2.5 %collective-permute-start.1 = (f32[2,512,128]{2,1,0:T(8,128)S(1)}, f32[2,512,128]{2,1,0:T(8,128)S(1)}, u32[]{:S(2)}, u32[]{:S(2)}) collective-permute-start(f32[2,512,128]{2,1,0:T(8,128)S(1)} %get-tuple-element.31), channel_id=1, source_target_pairs={{0,3},{1,0},{2,1},{3,2},{4,7},{5,4},{6,5},{7,6},{8,11},{9,8},{10,9... | collective-permute-start | bytes 1572872 | tf_op jit(solution)/shard_map/ppermute | solution.py:25
  5.3 0.7 collective-permute-start
  6.0 0.0 copy-done
  6.0 0.0 copy-done.1
  6.0 5.0 %patches_0.1 = (f32[2,6,768,128]{3,2,1,0:T(8,128)S(1)}, f32[2,6,768,128]{3,2,1,0:T(8,128)S(1)}, f32[2,256,256]{2,1,0:T(8,128)S(1)}, bf16[2,256,256]{2,1,0:T(8,128)(2,1)S(1)}, f32[2,2,256,128]{3,2,1,0:T(8,128)S(1)}) custom-call(s32[2,16]{1,0:T(2,128)S(1)} %bitcast.13, ...), custom_call_target="tpu_custom_call", output_to_operand_aliasing={{0}: (6, {}), {1}: (7, {}), {2}: (8, {})} | custom-call | flops 2147483648 | bytes 2097152 | tf_op jit(solution)/shard_map/patches_0/pallas_call | solution.py:349
  11.0 1.0 collective-permute-done.1.refs_1_
  12.0 1.7 %patches_1.1 = (f32[2,6,768,128]{3,2,1,0:T(8,128)S(1)}, f32[2,6,768,128]{3,2,1,0:T(8,128)S(1)}, f32[2,256,256]{2,1,0:T(8,128)S(1)}, bf16[2,256,256]{2,1,0:T(8,128)(2,1)S(1)}, f32[2,2,256,128]{3,2,1,0:T(8,128)S(1)}) custom-call(s32[2,16]{1,0:T(2,128)S(1)} %bitcast.14, ...), custom_call_target="tpu_custom_call", output_to_operand_aliasing={{0}: (7, {}), {1}: (8, {}), {2}: (9, {}), {3}: (10, {}), {4... | custom-call | flops 2147483648 | bytes 2097152 | tf_op jit(solution)/shard_map/patches_1/pallas_call | solution.py:349
  13.7 3.9 %collective-permute-done.refs_1_ = f32[2,512,128]{2,1,0:T(8,128)S(1)} collective-permute-done((f32[2,512,128]{2,1,0:T(8,128)S(1)}, f32[2,512,128]{2,1,0:T(8,128)S(1)}, u32[]{:S(2)}, u32[]{:S(2)}) %collective-permute-start) | collective-permute-done | bytes 524320 | tf_op jit(solution)/shard_map/ppermute | solution.py:25
  17.6 0.0 copy-start.2
  17.6 10.0 %patches_2.1 = (f32[2,6,768,128]{3,2,1,0:T(8,128)S(1)}, f32[2,6,768,128]{3,2,1,0:T(8,128)S(1)}, f32[2,256,256]{2,1,0:T(8,128)S(1)}, bf16[2,256,256]{2,1,0:T(8,128)(2,1)S(1)}, f32[2,2,256,128]{3,2,1,0:T(8,128)S(1)}) custom-call(s32[2,16]{1,0:T(2,128)S(1)} %bitcast.15, ...), custom_call_target="tpu_custom_call", output_to_operand_aliasing={{0}: (7, {}), {1}: (8, {}), {2}: (9, {}), {3}: (10, {}), {4... | custom-call | flops 2147483648 | bytes 2097152 | tf_op jit(solution)/shard_map/patches_2/pallas_call | solution.py:349
  27.6 0.0 copy-done.2
  27.6 95.0 %exchange.1 = f32[2,512,512]{2,1,0:T(8,128)S(1)} custom-call(f32[2,8,8]{2,1,0:T(8,128)S(1)} %copy-done.2, f32[2,6,768,128]{3,2,1,0:T(8,128)S(1)} %get-tuple-element.45.gradient, f32[2,6,768,128]{3,2,1,0:T(8,128)S(1)} %get-tuple-element.46.field, f32[2,2,256,128]{3,2,1,0:T(8,128)S(1)} %get-tuple-element.29.refs_4_.refs_5_.probe), custom_call_target="tpu_custom_call" | custom-call | tf_op jit(solution)/shard_map/exchange/pallas_call | solution.py:595
  122.6 1.3 %copy.36 = f32[1,2,1,512,512]{4,3,2,1,0:T(8,128)} copy(f32[1,2,1,512,512]{4,3,2,1,0:T(8,128)S(1)} %bitcast.12) | data formatting | bytes 4194304
Async XLA Ops:
  0.0 6.0 %copy-start = (bf16[1,1,16,256,256]{4,3,2,1,0:T(8,128)(2,1)S(1)}, bf16[1,1,16,256,256]{4,3,2,1,0:T(8,128)(2,1)}, u32[]{:S(2)}) copy-start(bf16[1,1,16,256,256]{4,3,2,1,0:T(8,128)(2,1)} %param.9) | copy-start | bytes 6291460
  0.0 6.0 %copy-start.1 = (s32[1,16,2]{1,2,0:T(2,128)S(1)}, s32[1,16,2]{1,2,0:T(2,128)}, u32[]{:S(2)}) copy-start(s32[1,16,2]{1,2,0:T(2,128)} %param.10) | copy-start | bytes 388
  2.8 9.2 %collective-permute-start.1 = (f32[2,512,128]{2,1,0:T(8,128)S(1)}, f32[2,512,128]{2,1,0:T(8,128)S(1)}, u32[]{:S(2)}, u32[]{:S(2)}) collective-permute-start(f32[2,512,128]{2,1,0:T(8,128)S(1)} %get-tuple-element.31), channel_id=1, source_target_pairs={{0,3},{1,0},{2,1},{3,2},{4,7},{5,4},{6,5},{7,6},{8,11},{9,8},{10,9... | collective-permute-start | bytes 1572872 | tf_op jit(solution)/shard_map/ppermute | solution.py:25
  5.3 12.3 %collective-permute-start = (f32[2,512,128]{2,1,0:T(8,128)S(1)}, f32[2,512,128]{2,1,0:T(8,128)S(1)}, u32[]{:S(2)}, u32[]{:S(2)}) collective-permute-start(f32[2,512,128]{2,1,0:T(8,128)S(1)} %get-tuple-element.26), channel_id=1, source_target_pairs={{0,3},{1,0},{2,1},{3,2},{4,7},{5,4},{6,5},{7,6},{8,11},{9,8},{10,9... | collective-permute-start | bytes 1572872 | tf_op jit(solution)/shard_map/ppermute | solution.py:25
  17.6 10.0 %copy-start.2 = (f32[2,8,8]{2,1,0:T(8,128)S(1)}, f32[2,8,8]{2,1,0:T(8,128)}, u32[]{:S(2)}) copy-start(f32[2,8,8]{2,1,0:T(8,128)} %materials_ref.1) | copy-start | bytes 1540
